TPU v7x, 128 devices: a whole 4x4x4 slice. The times are simulated.
128 devices in a mesh: dom: 64 (over x, z, y), batch: 2 (over core).
Axes of the slice: x: 4, y: 4, z: 4, core: 2. Of those that a mesh axis runs over, the one named last changes fastest.
Arguments:
- features: bfloat16 [4, 65536, 512], P('batch', 'dom'), may hold values from -6 to 6
- tile_vals: bfloat16 [2048, 128, 128], P('dom'), may hold values from -0.25 to 0.25
- tile_row: int32 [2048], P('dom'), may hold values from 0 to 7
- tile_col: int32 [2048], P('dom'), may hold values from 0 to 11
- send_next: int32 [128], P('dom'), may hold values from 0 to 7
- send_prev: int32 [128], P('dom'), may hold values from 0 to 7
- cluster: int32 [65536], P('dom'), may hold values from 0 to 1023, as said below
- cotangent: bfloat16 [4, 65536, 512], P('batch', 'dom'), may hold values from -6 to 6
- self_weight: bfloat16 [512, 512], replicated, may hold values from -0.25 to 0.25
- neighbour_weight: bfloat16 [512, 512], replicated, may hold values from -0.25 to 0.25
- w_coarse: bfloat16 [512, 512], replicated, may hold values from -0.25 to 0.25
Outputs:
- output: bfloat16 [4, 65536, 512], P('batch', 'dom')
- self_weight_gradient: float32 [512, 512], replicated
- neighbour_weight_gradient: float32 [512, 512], replicated
- grad_coarse: float32 [512, 512], replicated
Inputs may be any that keep to these rules, and one draw needn't show every extreme that they name: Within each pair of partitions 2m, 2m + 1, every cluster number names exactly two of the pair's 2 * 1024 nodes.
All inputs are finite; a program needn't handle non-finite values.
Results may differ from a plain program's by a relative error of at most 0.012.
Values may be sent and summed in bfloat16 or wider, within the bound.
A program may use at most 128 MiB of HBM per device.

v0:
```python
import math
import jax
import jax.numpy as jnp
from jax import lax
from jax.sharding import PartitionSpec as P


def shifted(x, axis, by):
    length = lax.axis_size(axis)
    pairs = [(i, i + by) for i in range(length) if 0 <= i + by < length]
    return lax.ppermute(x, axis, pairs)


def partner(value, axis, distance):
    mask = 2**distance
    pairs = [(source, source ^ mask) for source in range(lax.axis_size(axis))]
    return lax.ppermute(value, axis, pairs)


def dsilu(value):
    sig = jax.nn.sigmoid(value)
    return sig * (1.0 + value * (1.0 - sig))


def member_table(labels, count):
    return (labels[None, :] == jnp.arange(count, dtype=jnp.int32)[:, None]).astype(jnp.bfloat16)


def pooling(rows, table):
    return jnp.einsum("cn,snd->scd", table, rows, preferred_element_type=jnp.float32)


def lookup(coarse_rows, table):
    return jnp.einsum("cn,scd->snd", table, coarse_rows, preferred_element_type=jnp.float32)


def pick_blocks(labels, count, tiled):
    table = (labels[:, None] == jnp.arange(count, dtype=jnp.int32)[None, :]).astype(jnp.bfloat16)
    return jnp.einsum("tb,sbjd->stjd", table, tiled, preferred_element_type=jnp.float32).astype(
        jnp.bfloat16
    )


def local(
    features,
    tile_vals,
    tile_row,
    tile_col,
    send_next,
    send_prev,
    cluster,
    cotangent,
    self_weight,
    neighbour_weight,
    w_coarse,
):
    scen, nodes, width = features.shape
    side = tile_vals.shape[1]
    blocks = nodes // side
    tiled = features.reshape(scen, blocks, side, width)
    to_next = pick_blocks(send_next, blocks, tiled)
    to_prev = pick_blocks(send_prev, blocks, tiled)
    got_prev = shifted(to_next, "dom", 1)
    got_next = shifted(to_prev, "dom", -1)
    extended = jnp.concatenate([tiled, got_prev, got_next], axis=1)
    picked = pick_blocks(tile_col, extended.shape[1], extended)
    terms = jnp.einsum("tij,stjd->stid", tile_vals, picked, preferred_element_type=jnp.float32)
    rowhot = (tile_row[None, :] == jnp.arange(blocks, dtype=jnp.int32)[:, None]).astype(jnp.float32)
    summed = jnp.einsum("rt,stid->srid", rowhot, terms, precision=lax.Precision.HIGHEST)
    neighbour_total = summed.reshape(scen, nodes, width).astype(jnp.bfloat16)
    preactivation = jnp.einsum(
        "jkb,bt->jkt", features, self_weight, preferred_element_type=jnp.float32
    )
    preactivation = preactivation + jnp.einsum(
        "jkb,bt->jkt", neighbour_total, neighbour_weight, preferred_element_type=jnp.float32
    )
    hidden = jax.nn.silu(preactivation).astype(jnp.bfloat16)
    table = member_table(cluster, nodes)
    parity = lax.axis_index("dom") % 2
    half = nodes // 2
    own_start = parity * half

    def owned(array):
        return lax.dynamic_slice_in_dim(array, own_start, half, 1)

    partial_value = pooling(hidden, table)
    grad_partial = pooling(cotangent, table)
    partner_sums = partner(partial_value.astype(jnp.bfloat16), "dom", 0).astype(partial_value.dtype)
    coarse = (0.5 * (partial_value + partner_sums)).astype(jnp.bfloat16)
    act = jnp.einsum("skd,de->ske", coarse, w_coarse, preferred_element_type=jnp.float32)
    lifted = jax.nn.silu(act).astype(jnp.bfloat16)
    grad_lift = grad_partial + partner(grad_partial.astype(jnp.bfloat16), "dom", 0).astype(
        grad_partial.dtype
    )
    grad_act = (grad_lift * dsilu(act)).astype(jnp.bfloat16)
    term_coarse = jnp.einsum(
        "skd,ske->de", owned(coarse), owned(grad_act), preferred_element_type=jnp.float32
    )
    grad_down = jnp.einsum(
        "ske,de->skd", grad_act, w_coarse, preferred_element_type=jnp.float32
    ).astype(jnp.bfloat16)
    spread = lookup(lifted, table)
    output = (hidden.astype(jnp.float32) + spread).astype(jnp.bfloat16)
    back = lookup(grad_down, table)
    grad_hidden = cotangent.astype(jnp.float32) + 0.5 * back
    preactivation_gradient = (grad_hidden * dsilu(preactivation)).astype(jnp.bfloat16)
    self_contribution = jnp.einsum(
        "btv,btq->vq", features, preactivation_gradient, preferred_element_type=jnp.float32
    )
    neighbour_contribution = jnp.einsum(
        "btv,btq->vq", neighbour_total, preactivation_gradient, preferred_element_type=jnp.float32
    )
    totals = lax.psum((self_contribution, neighbour_contribution, term_coarse), ("dom", "batch"))
    gradient_scale = 1.0 / math.sqrt(scen * lax.axis_size("batch") * nodes * lax.axis_size("dom"))
    return (
        output,
        totals[0] * gradient_scale,
        totals[1] * gradient_scale,
        totals[2] * gradient_scale,
    )


def solution(mesh):
    in_specs = (
        P("batch", "dom", None),
        P("dom", None, None),
        P("dom"),
        P("dom"),
        P("dom"),
        P("dom"),
        P("dom"),
        P("batch", "dom", None),
        P(),
        P(),
        P(),
    )
    out_specs = (P("batch", "dom", None), P(), P(), P())
    return jax.shard_map(local, mesh=mesh, in_specs=in_specs, out_specs=out_specs, check_vma=False)
```

profile of v0, /device:TPU:1, one launch (start us, length us, event | category | flops | bytes accessed | tf_op | source)
XLA Modules:
  0.0 384.3 jit_solution(13734323582045857980)
XLA Ops:
  7.2 3.2 fusion.35
  10.5 4.1 %collective-permute-start = (bf16[2,2,128,512]{3,1,2,0:T(2,128)(2,1)S(1)}, bf16[2,2,128,512]{3,1,2,0:T(2,128)(2,1)S(1)}, u32[]{:S(2)}, u32[]{:S(2)}) collective-permute-start(bf16[2,2,128,512]{3,1,2,0:T(2,128)(2,1)S(1)} %fusion.35), channel_id=1, source_target_pairs={{0,2},{2,4},{4,6},{6,8},{8,10},{10,12},{12,14},{14,16},{16,18},{18... | collective-permute-start | bytes 1572872 | tf_op jit(solution)/shard_map/ppermute | solution.py:11
  14.5 3.1 fusion.36
  17.6 1.3 collective-permute-start.1
  18.9 1.2 copy.58
  20.1 3.3 fusion.45
  23.4 1.7 collective-permute-done
  25.1 6.9 %collective-permute-done.1 = bf16[2,2,128,512]{3,1,2,0:T(2,128)(2,1)S(1)} collective-permute-done((bf16[2,2,128,512]{3,1,2,0:T(2,128)(2,1)S(1)}, bf16[2,2,128,512]{3,1,2,0:T(2,128)(2,1)S(1)}, u32[]{:S(2)}, u32[]{:S(2)}) %collective-permute-start.1) | collective-permute-done | bytes 524320 | tf_op jit(solution)/shard_map/ppermute | solution.py:11
  32.0 5.3 %convert_bitcast_fusion = bf16[2,32,128,512]{3,1,2,0:T(8,128)(2,1)} fusion(bf16[2,2,128,512]{3,1,2,0:T(2,128)(2,1)S(1)} %collective-permute-done.1, bf16[2,2,128,512]{3,1,2,0:T(2,128)(2,1)S(1)} %collective-permute-done, bf16[2,8,128,512]{3,1,2,0:T(8,128)(2,1)S(1)} %copy.58, s32[32]{0:T(128)S(1)} %copy-done.15), kind=kOutput, calls=%fused_computation.2 | convolution fusion | flops 114295168 | bytes 11534464 | tf_op jit(solution)/shard_map/tb,sbjd->stjd/dot_general | solution.py:39
  37.3 18.5 %convolution_bitcast_fusion = f32[2,32,128,512]{2,3,0,1:T(8,128)} fusion(bf16[2,32,128,512]{3,1,2,0:T(8,128)(2,1)} %convert_bitcast_fusion, bf16[32,128,128]{2,1,0:T(8,128)(2,1)S(1)} %copy-done), kind=kOutput, calls=%fused_computation | convolution fusion | flops 1073741824 | bytes 26214400 | tf_op jit(solution)/shard_map/tij,stjd->stid/dot_general | solution.py:67
  55.8 20.1 %copy.60 = f32[2,32,128,512]{3,1,2,0:T(8,128)} copy(f32[2,32,128,512]{2,3,0,1:T(8,128)} %convolution_bitcast_fusion) | data formatting | bytes 33554432 | tf_op jit(solution)/shard_map/tij,stjd->stid/transpose | solution.py:67
  75.9 9.2 %convert_bitcast_fusion.1 = bf16[2,8,128,512]{3,1,2,0:T(8,128)(2,1)S(1)} fusion(f32[2,32,128,512]{3,1,2,0:T(8,128)} %copy.60, s32[32]{0:T(128)S(1)} %copy-done.11), kind=kOutput, calls=%fused_computation.37 | convolution fusion | flops 403702016 | bytes 18874496 | tf_op jit(solution)/shard_map/rt,stid->srid/dot_general | solution.py:69
  85.8 1.3 copy-done.4
  88.1 1.2 convolution_add_fusion
  89.3 5.5 %bitcast_convert_fusion.1 = (bf16[2,1024,512]{1,2,0:T(8,128)(2,1)}, f32[2,512,1024]{2,1,0:T(8,128)}) fusion(s32[1024]{0:T(1024)S(1)} %copy-done.14, f32[2,1024,512]{2,1,0:T(8,128)S(1)} %convolution_add_fusion), kind=kOutput, calls=%fused_computation.18 | convolution fusion | flops 2154823680 | bytes 10489856 | tf_op jit(solution)/shard_map/cn,snd->scd/dot_general | solution.py:30
  94.8 1.3 collective-permute-start.2
  96.1 5.0 %bitcast_convert_fusion = (bf16[2,1024,512]{2,1,0:T(8,128)(2,1)}, f32[1024,2,512]{2,0,1:T(8,128)}) fusion(bf16[2,1024,512]{2,1,0:T(8,128)(2,1)S(1)} %copy-done.12, s32[1024]{0:T(1024)S(1)} %copy-done.14), kind=kOutput, calls=%fused_computation.12 | convolution fusion | flops 2149580800 | bytes 8392704 | tf_op jit(solution)/shard_map/cn,snd->scd/dot_general | solution.py:30
  101.5 38.9 %collective-permute-done.2 = bf16[2,1024,512]{1,2,0:T(8,128)(2,1)} collective-permute-done((bf16[2,1024,512]{1,2,0:T(8,128)(2,1)}, bf16[2,1024,512]{1,2,0:T(8,128)(2,1)}, u32[]{:S(2)}, u32[]{:S(2)}) %collective-permute-start.2) | collective-permute-done | bytes 2097184 | tf_op jit(solution)/shard_map/ppermute | solution.py:17
  140.4 3.8 fusion.12
  144.2 41.1 %collective-permute-done.3 = bf16[2,1024,512]{2,1,0:T(8,128)(2,1)} collective-permute-done((bf16[2,1024,512]{2,1,0:T(8,128)(2,1)}, bf16[2,1024,512]{2,1,0:T(8,128)(2,1)}, u32[]{:S(2)}, u32[]{:S(2)}) %collective-permute-start.3) | collective-permute-done | bytes 2097184 | tf_op jit(solution)/shard_map/ppermute | solution.py:17
  185.3 6.8 %fusion.9 = (bf16[2,1024,512]{2,1,0:T(8,128)(2,1)}, f32[2,1024,512]{2,1,0:T(8,128)}) fusion(f32[1024,2,512]{2,0,1:T(8,128)S(1)} %copy-done.17, bf16[2,1024,512]{2,1,0:T(8,128)(2,1)} %collective-permute-done.3, bf16[2,1024,512]{1,2,0:T(8,128)(2,1)S(1)} %fusion.12, bf16[512,512]{1,0:T(8,128)(2,1)S(1)} %copy-done.13), kind=kOutput, calls=%fused_computation.14 | convolution fusion | flops 1085276160 | bytes 15204352 | tf_op jit(solution)/shard_map/skd,de->ske/dot_general | solution.py:90
  192.1 8.1 %fusion.7 = bf16[2,1024,512]{2,1,0:T(8,128)(2,1)} fusion(f32[2,1024,512]{2,1,0:T(8,128)} %copy-done.5, bf16[2,1024,512]{2,1,0:T(8,128)(2,1)} %param.18, s32[1024]{0:T(1024)S(1)} %copy-done.14, bf16[2,1024,512]{2,1,0:T(8,128)(2,1)} %get-tuple-element.27, bf16[512,512]{1,0:T(8,128)(2,1)S(1)} %copy-done.13), kind=kOutput, calls=%fused_computation.10 | convolution fusion | flops 3235905536 | bytes 11014144 | tf_op jit(solution)/shard_map/cn,scd->snd/dot_general | solution.py:34
  200.2 4.6 %convolution_bitcast_fusion.2 = f32[512,512]{0,1:T(8,128)} fusion(bf16[2,1024,512]{2,1,0:T(8,128)(2,1)} %bitcast.111, bf16[2,1024,512]{2,1,0:T(8,128)(2,1)} %fusion.7), kind=kOutput, calls=%fused_computation.40 | convolution fusion | flops 1073741824 | bytes 5242880 | tf_op jit(solution)/shard_map/btv,btq->vq/dot_general | solution.py:110
  204.8 2.2 convolution_bitcast_fusion.3
  207.0 1.7 convolution_bitcast_fusion.1
  208.8 8.0 %fusion.10 = bf16[2,1024,512]{2,1,0:T(8,128)(2,1)} fusion(s32[1024]{0:T(1024)S(1)} %copy-done.14, f32[2,1024,512]{2,1,0:T(8,128)} %get-tuple-element.28, f32[2,1024,512]{2,1,0:T(8,128)} %copy-done.5), kind=kOutput, calls=%fused_computation.16 | convolution fusion | flops 2162163712 | bytes 10489856 | tf_op jit(solution)/shard_map/cn,scd->snd/dot_general | solution.py:34
  216.8 153.4 %all-reduce.3.cloned.1.call-done = (f32[512,512]{0,1:T(8,128)}, f32[512,512]{0,1:T(8,128)}, f32[512,512]{0,1:T(8,128)}) async-done(((f32[512,512]{0,1:T(8,128)}, f32[512,512]{0,1:T(8,128)}, f32[512,512]{0,1:T(8,128)}), (f32[512,512]{0,1:T(8,128)}, f32[512,512]{0,1:T(8,128)}, f32[512,512]{0,1:T(8,128)})) %all-reduce.3.cloned.1.call-update) | async-done | bytes 3145744 | tf_op jit(solution)/shard_map/psum | solution.py:113
  370.2 1.8 broadcast_multiply_fusion
  372.0 1.3 copy.73
  373.3 1.3 copy.74
  374.6 1.3 broadcast_multiply_fusion.2
  375.9 1.3 copy.72
  (39 shorter events, 2.1 us)
Async XLA Ops:
  7.2 30.1 %copy-start = (bf16[32,128,128]{2,1,0:T(8,128)(2,1)S(1)}, bf16[32,128,128]{2,1,0:T(8,128)(2,1)}, u32[]{:S(2)}) copy-start(bf16[32,128,128]{2,1,0:T(8,128)(2,1)} %param.12) | copy-start | bytes 3145732
  7.2 11.7 %copy-start.2 = (bf16[2,1024,512]{2,1,0:T(8,128)(2,1)S(1)}, bf16[2,1024,512]{2,1,0:T(8,128)(2,1)}, u32[]{:S(2)}) copy-start(bf16[2,1024,512]{2,1,0:T(8,128)(2,1)} %param.11) | copy-start | bytes 6291460
  7.2 363.0 %all-reduce.3.cloned.1.call-start = ((), (), s32[]{:S(2)}) async-start(), calls=%async_computation | async-start | bytes 6291456 | tf_op jit(solution)/shard_map/psum | solution.py:113
  7.2 12.8 %copy-start.9 = (bf16[512,512]{1,0:T(8,128)(2,1)S(1)}, bf16[512,512]{1,0:T(8,128)(2,1)}, u32[]{:S(2)}) copy-start(bf16[512,512]{1,0:T(8,128)(2,1)} %param.19) | copy-start | bytes 1572868
  10.5 14.6 %collective-permute-start = (bf16[2,2,128,512]{3,1,2,0:T(2,128)(2,1)S(1)}, bf16[2,2,128,512]{3,1,2,0:T(2,128)(2,1)S(1)}, u32[]{:S(2)}, u32[]{:S(2)}) collective-permute-start(bf16[2,2,128,512]{3,1,2,0:T(2,128)(2,1)S(1)} %fusion.35), channel_id=1, source_target_pairs={{0,2},{2,4},{4,6},{6,8},{8,10},{10,12},{12,14},{14,16},{16,18},{18... | collective-permute-start | bytes 1572872 | tf_op jit(solution)/shard_map/ppermute | solution.py:11
  17.6 14.4 %collective-permute-start.1 = (bf16[2,2,128,512]{3,1,2,0:T(2,128)(2,1)S(1)}, bf16[2,2,128,512]{3,1,2,0:T(2,128)(2,1)S(1)}, u32[]{:S(2)}, u32[]{:S(2)}) collective-permute-start(bf16[2,2,128,512]{3,1,2,0:T(2,128)(2,1)S(1)} %fusion.36), channel_id=1, source_target_pairs={{2,0},{4,2},{6,4},{8,6},{10,8},{12,10},{14,12},{16,14},{18,16},{20... | collective-permute-start | bytes 1572872 | tf_op jit(solution)/shard_map/ppermute | solution.py:11
  20.1 11.9 %copy-start.15 = (s32[32]{0:T(128)S(1)}, s32[32]{0:T(128)}, u32[]{:S(2)}) copy-start(s32[32]{0:T(128)} %param.14) | copy-start | bytes 388
  55.8 20.1 %copy-start.11 = (s32[32]{0:T(128)S(1)}, s32[32]{0:T(128)}, u32[]{:S(2)}) copy-start(s32[32]{0:T(128)} %param.13) | copy-start | bytes 388
  75.8 11.3 %copy-start.10 = (bf16[512,512]{1,0:T(8,128)(2,1)S(1)}, bf16[512,512]{1,0:T(8,128)(2,1)}, u32[]{:S(2)}) copy-start(bf16[512,512]{1,0:T(8,128)(2,1)} %param.20) | copy-start | bytes 1572868
  85.1 2.9 copy-start.3
  85.8 1.3 copy-start.4
  88.1 1.3 copy-start.14
  89.3 5.5 %copy-start.5 = (f32[2,1024,512]{2,1,0:T(8,128)}, f32[2,1024,512]{2,1,0:T(8,128)S(1)}, u32[]{:S(2)}) copy-start(f32[2,1024,512]{2,1,0:T(8,128)S(1)} %convolution_add_fusion) | copy-start | bytes 12582916
  89.3 6.8 %copy-start.12 = (bf16[2,1024,512]{2,1,0:T(8,128)(2,1)S(1)}, bf16[2,1024,512]{2,1,0:T(8,128)(2,1)}, u32[]{:S(2)}) copy-start(bf16[2,1024,512]{2,1,0:T(8,128)(2,1)} %param.18) | copy-start | bytes 6291460
  94.8 45.6 %collective-permute-start.2 = (bf16[2,1024,512]{1,2,0:T(8,128)(2,1)}, bf16[2,1024,512]{1,2,0:T(8,128)(2,1)}, u32[]{:S(2)}, u32[]{:S(2)}) collective-permute-start(bf16[2,1024,512]{1,2,0:T(8,128)(2,1)} %get-tuple-element.23), channel_id=1, source_target_pairs={{0,2},{2,0},{4,6},{6,4},{8,10},{10,8},{12,14},{14,12},{16,18},{18,... | collective-permute-start | bytes 6291464 | tf_op jit(solution)/shard_map/ppermute | solution.py:17
  101.1 84.2 %collective-permute-start.3 = (bf16[2,1024,512]{2,1,0:T(8,128)(2,1)}, bf16[2,1024,512]{2,1,0:T(8,128)(2,1)}, u32[]{:S(2)}, u32[]{:S(2)}) collective-permute-start(bf16[2,1024,512]{2,1,0:T(8,128)(2,1)} %get-tuple-element.25), channel_id=1, source_target_pairs={{0,2},{2,0},{4,6},{6,4},{8,10},{10,8},{12,14},{14,12},{16,18},{18,... | collective-permute-start | bytes 6291464 | tf_op jit(solution)/shard_map/ppermute | solution.py:17
  140.4 44.9 %copy-start.13 = (bf16[512,512]{1,0:T(8,128)(2,1)S(1)}, bf16[512,512]{1,0:T(8,128)(2,1)}, u32[]{:S(2)}) copy-start(bf16[512,512]{1,0:T(8,128)(2,1)} %param.21) | copy-start | bytes 1572868
  140.4 44.9 %copy-start.17 = (f32[1024,2,512]{2,0,1:T(8,128)S(1)}, f32[1024,2,512]{2,0,1:T(8,128)}, u32[]{:S(2)}) copy-start(f32[1024,2,512]{2,0,1:T(8,128)} %get-tuple-element.26) | copy-start | bytes 12582916
  144.2 47.9 %copy-start.7 = (bf16[2,1024,512]{1,2,0:T(8,128)(2,1)}, bf16[2,1024,512]{1,2,0:T(8,128)(2,1)S(1)}, u32[]{:S(2)}) copy-start(bf16[2,1024,512]{1,2,0:T(8,128)(2,1)S(1)} %fusion.12) | copy-start | bytes 6291460
  200.2 4.6 %copy-start.6 = (bf16[2,1024,512]{2,1,0:T(8,128)(2,1)S(1)}, bf16[2,1024,512]{2,1,0:T(8,128)(2,1)}, u32[]{:S(2)}) copy-start(bf16[2,1024,512]{2,1,0:T(8,128)(2,1)} %fusion.7) | copy-start | bytes 6291460
  204.8 2.2 copy-start.8
  204.8 2.2 copy-start.16
  371.9 5.3 %copy-start.1 = (bf16[32,128,128]{2,1,0:T(8,128)(2,1)S(1)}, bf16[32,128,128]{2,1,0:T(8,128)(2,1)}, u32[]{:S(2)}) copy-start(bf16[32,128,128]{2,1,0:T(8,128)(2,1)} %param.12) | copy-start | bytes 3145732
Sparse Core Ops, SparseCore 0:
  208.9 161.1 all-reduce.2
where the time goes:
time: 389 us; the launch traced here: 384 us
  waiting for transfers between devices  242 us (62%)
  matrix products  85.8 us (22%)
  local copies, waits for them, and re-layouts  28.1 us (7%)
  between operations  14.5 us (4%)
  starting transfers between devices  7.05 us (2%)
  other arithmetic  6.86 us (2%)
    psum x1, waiting for transfers between devices, local(): lax.psum((self_contribution, neighbour_contribution, term_coarse), ('dom'...  153 us
    ppermute x2, waiting for transfers between devices, partner(): return lax.ppermute(value, axis, pairs)  80 us
    transpose x1, local copies, waits for them, and re-layouts, local(): jnp.einsum('tij,stjd->stid', tile_vals, picked, preferred_element_type=jn...  20.1 us
    dot_general x1, matrix products, local(): jnp.einsum('tij,stjd->stid', tile_vals, picked, preferred_element_type=jn...  18.5 us
    dot_general x2, matrix products, lookup(): jnp.einsum('cn,scd->snd', table, coarse_rows, preferred_element_type=jnp....  16.1 us
    dot_general x3, matrix products, pick_blocks(): jnp.einsum('tb,sbjd->stjd', table, tiled, preferred_element_type=jnp.floa...  11.6 us
    dot_general x2, matrix products, pooling(): jnp.einsum('cn,snd->scd', table, rows, preferred_element_type=jnp.float32)  10.5 us
    dot_general x1, matrix products, local(): jnp.einsum('rt,stid->srid', rowhot, terms, precision=lax.Precision.HIGHEST)  9.25 us
  transfers between devices with their start and end apart: 5, of which 5 were waited for; matrix products, arithmetic and copies ran while one was open for 6% of the time, Pallas kernels for 0%

commit v1 on v0

--- a/solution.py
+++ b/solution.py
@@ -110,7 +110,9 @@
     neighbour_contribution = jnp.einsum(
         "btv,btq->vq", neighbour_total, preactivation_gradient, preferred_element_type=jnp.float32
     )
-    totals = lax.psum((self_contribution, neighbour_contribution, term_coarse), ("dom", "batch"))
+    totals = (self_contribution, neighbour_contribution, term_coarse)
+    for kk in ("dom", "batch"):
+        totals = lax.psum(totals, kk)
     gradient_scale = 1.0 / math.sqrt(scen * lax.axis_size("batch") * nodes * lax.axis_size("dom"))
     return (
         output,

time: 389 us -> 402 us (1.033)
  waiting for transfers between devices: 242 us -> 255 us
    psum x1 -> x2, waiting for transfers between devices: 153 us -> 166 us  [local(): totals = lax.psum(totals, kk)]
  transfers between devices with their start and end apart: 5 -> 6, of which waited for: 5 -> 6; matrix products, arithmetic and copies ran while one was open for 6% -> 6% of each run, Pallas kernels for 0% -> 0%
where the time goes in v1:
time: 402 us; the launch traced here: 397 us
  waiting for transfers between devices  255 us (63%)
  matrix products  86 us (21%)
  local copies, waits for them, and re-layouts  28.1 us (7%)
  between operations  14.5 us (4%)
  starting transfers between devices  7.26 us (2%)
  other arithmetic  6.86 us (2%)
    psum x2, waiting for transfers between devices, local(): totals = lax.psum(totals, kk)  166 us
    ppermute x2, waiting for transfers between devices, partner(): return lax.ppermute(value, axis, pairs)  80.1 us
    transpose x1, local copies, waits for them, and re-layouts, local(): jnp.einsum('tij,stjd->stid', tile_vals, picked, preferred_element_type=jn...  20 us
    dot_general x1, matrix products, local(): jnp.einsum('tij,stjd->stid', tile_vals, picked, preferred_element_type=jn...  18.5 us
    dot_general x2, matrix products, lookup(): jnp.einsum('cn,scd->snd', table, coarse_rows, preferred_element_type=jnp....  16.1 us
    dot_general x3, matrix products, pick_blocks(): jnp.einsum('tb,sbjd->stjd', table, tiled, preferred_element_type=jnp.floa...  11.4 us
    dot_general x2, matrix products, pooling(): jnp.einsum('cn,snd->scd', table, rows, preferred_element_type=jnp.float32)  10.5 us
    dot_general x1, matrix products, local(): jnp.einsum('rt,stid->srid', rowhot, terms, precision=lax.Precision.HIGHEST)  9.57 us
  transfers between devices with their start and end apart: 6, of which 6 were waited for; matrix products, arithmetic and copies ran while one was open for 6% of the time, Pallas kernels for 0%

profile of v1, /device:TPU:1, one launch (start us, length us, event | category | flops | bytes accessed | tf_op | source)
XLA Modules:
  0.0 397.2 jit_solution(7552107408937285622)
XLA Ops:
  7.2 3.2 fusion.35
  10.5 4.1 %collective-permute-start = (bf16[2,2,128,512]{3,1,2,0:T(2,128)(2,1)S(1)}, bf16[2,2,128,512]{3,1,2,0:T(2,128)(2,1)S(1)}, u32[]{:S(2)}, u32[]{:S(2)}) collective-permute-start(bf16[2,2,128,512]{3,1,2,0:T(2,128)(2,1)S(1)} %fusion.35), channel_id=1, source_target_pairs={{0,2},{2,4},{4,6},{6,8},{8,10},{10,12},{12,14},{14,16},{16,18},{18... | collective-permute-start | bytes 1572872 | tf_op jit(solution)/shard_map/ppermute | solution.py:11
  14.5 3.1 fusion.36
  17.6 1.3 collective-permute-start.1
  20.1 3.3 fusion.45
  23.4 1.7 collective-permute-done
  25.1 6.9 %collective-permute-done.1 = bf16[2,2,128,512]{3,1,2,0:T(2,128)(2,1)S(1)} collective-permute-done((bf16[2,2,128,512]{3,1,2,0:T(2,128)(2,1)S(1)}, bf16[2,2,128,512]{3,1,2,0:T(2,128)(2,1)S(1)}, u32[]{:S(2)}, u32[]{:S(2)}) %collective-permute-start.1) | collective-permute-done | bytes 524320 | tf_op jit(solution)/shard_map/ppermute | solution.py:11
  32.0 5.1 %convert_bitcast_fusion = bf16[2,32,128,512]{3,1,2,0:T(8,128)(2,1)} fusion(bf16[2,2,128,512]{3,1,2,0:T(2,128)(2,1)S(1)} %collective-permute-done.1, bf16[2,2,128,512]{3,1,2,0:T(2,128)(2,1)S(1)} %collective-permute-done, bf16[2,8,128,512]{3,1,2,0:T(8,128)(2,1)S(1)} %copy.58, s32[32]{0:T(128)S(1)} %copy-done.15), kind=kOutput, calls=%fused_computation.2 | convolution fusion | flops 114295168 | bytes 11534464 | tf_op jit(solution)/shard_map/tb,sbjd->stjd/dot_general | solution.py:39
  37.1 18.5 %convolution_bitcast_fusion = f32[2,32,128,512]{2,3,0,1:T(8,128)} fusion(bf16[2,32,128,512]{3,1,2,0:T(8,128)(2,1)} %convert_bitcast_fusion, bf16[32,128,128]{2,1,0:T(8,128)(2,1)S(1)} %copy-done), kind=kOutput, calls=%fused_computation | convolution fusion | flops 1073741824 | bytes 26214400 | tf_op jit(solution)/shard_map/tij,stjd->stid/dot_general | solution.py:67
  55.6 20.0 %copy.60 = f32[2,32,128,512]{3,1,2,0:T(8,128)} copy(f32[2,32,128,512]{2,3,0,1:T(8,128)} %convolution_bitcast_fusion) | data formatting | bytes 33554432 | tf_op jit(solution)/shard_map/tij,stjd->stid/transpose | solution.py:67
  75.6 9.6 %convert_bitcast_fusion.1 = bf16[2,8,128,512]{3,1,2,0:T(8,128)(2,1)S(1)} fusion(f32[2,32,128,512]{3,1,2,0:T(8,128)} %copy.60, s32[32]{0:T(128)S(1)} %copy-done.11), kind=kOutput, calls=%fused_computation.37 | convolution fusion | flops 403702016 | bytes 18874496 | tf_op jit(solution)/shard_map/rt,stid->srid/dot_general | solution.py:69
  85.9 1.3 copy-done.4
  88.1 1.2 convolution_add_fusion
  89.4 5.5 %bitcast_convert_fusion.1 = (bf16[2,1024,512]{1,2,0:T(8,128)(2,1)}, f32[2,512,1024]{2,1,0:T(8,128)}) fusion(s32[1024]{0:T(1024)S(1)} %copy-done.14, f32[2,1024,512]{2,1,0:T(8,128)S(1)} %convolution_add_fusion), kind=kOutput, calls=%fused_computation.18 | convolution fusion | flops 2154823680 | bytes 10489856 | tf_op jit(solution)/shard_map/cn,snd->scd/dot_general | solution.py:30
  94.9 1.3 collective-permute-start.2
  96.1 5.0 %bitcast_convert_fusion = (bf16[2,1024,512]{2,1,0:T(8,128)(2,1)}, f32[1024,2,512]{2,0,1:T(8,128)}) fusion(bf16[2,1024,512]{2,1,0:T(8,128)(2,1)S(1)} %copy-done.12, s32[1024]{0:T(1024)S(1)} %copy-done.14), kind=kOutput, calls=%fused_computation.12 | convolution fusion | flops 2149580800 | bytes 8392704 | tf_op jit(solution)/shard_map/cn,snd->scd/dot_general | solution.py:30
  101.5 38.9 %collective-permute-done.2 = bf16[2,1024,512]{1,2,0:T(8,128)(2,1)} collective-permute-done((bf16[2,1024,512]{1,2,0:T(8,128)(2,1)}, bf16[2,1024,512]{1,2,0:T(8,128)(2,1)}, u32[]{:S(2)}, u32[]{:S(2)}) %collective-permute-start.2) | collective-permute-done | bytes 2097184 | tf_op jit(solution)/shard_map/ppermute | solution.py:17
  140.4 3.8 fusion.12
  144.2 41.1 %collective-permute-done.3 = bf16[2,1024,512]{2,1,0:T(8,128)(2,1)} collective-permute-done((bf16[2,1024,512]{2,1,0:T(8,128)(2,1)}, bf16[2,1024,512]{2,1,0:T(8,128)(2,1)}, u32[]{:S(2)}, u32[]{:S(2)}) %collective-permute-start.3) | collective-permute-done | bytes 2097184 | tf_op jit(solution)/shard_map/ppermute | solution.py:17
  185.4 6.7 %fusion.9 = (bf16[2,1024,512]{2,1,0:T(8,128)(2,1)}, f32[2,1024,512]{2,1,0:T(8,128)}) fusion(f32[1024,2,512]{2,0,1:T(8,128)S(1)} %copy-done.17, bf16[2,1024,512]{2,1,0:T(8,128)(2,1)} %collective-permute-done.3, bf16[2,1024,512]{1,2,0:T(8,128)(2,1)S(1)} %fusion.12, bf16[512,512]{1,0:T(8,128)(2,1)S(1)} %copy-done.13), kind=kOutput, calls=%fused_computation.14 | convolution fusion | flops 1085276160 | bytes 15204352 | tf_op jit(solution)/shard_map/skd,de->ske/dot_general | solution.py:90
  192.1 8.1 %fusion.7 = bf16[2,1024,512]{2,1,0:T(8,128)(2,1)} fusion(f32[2,1024,512]{2,1,0:T(8,128)} %copy-done.5, bf16[2,1024,512]{2,1,0:T(8,128)(2,1)} %param.18, s32[1024]{0:T(1024)S(1)} %copy-done.14, bf16[2,1024,512]{2,1,0:T(8,128)(2,1)} %get-tuple-element.30, bf16[512,512]{1,0:T(8,128)(2,1)S(1)} %copy-done.13), kind=kOutput, calls=%fused_computation.10 | convolution fusion | flops 3235905536 | bytes 11014144 | tf_op jit(solution)/shard_map/cn,scd->snd/dot_general | solution.py:34
  200.2 4.6 %convolution_bitcast_fusion.2 = f32[512,512]{0,1:T(8,128)} fusion(bf16[2,1024,512]{2,1,0:T(8,128)(2,1)} %bitcast.111, bf16[2,1024,512]{2,1,0:T(8,128)(2,1)} %fusion.7), kind=kOutput, calls=%fused_computation.40 | convolution fusion | flops 1073741824 | bytes 5242880 | tf_op jit(solution)/shard_map/btv,btq->vq/dot_general | solution.py:110
  204.9 2.2 convolution_bitcast_fusion.3
  207.1 1.7 convolution_bitcast_fusion.1
  209.1 142.5 %all-reduce.5.cloned.1.call-done = (f32[512,512]{0,1:T(8,128)}, f32[512,512]{0,1:T(8,128)}, f32[512,512]{0,1:T(8,128)}) async-done(((f32[512,512]{0,1:T(8,128)}, f32[512,512]{0,1:T(8,128)}, f32[512,512]{0,1:T(8,128)}), (f32[512,512]{0,1:T(8,128)}, f32[512,512]{0,1:T(8,128)}, f32[512,512]{0,1:T(8,128)})) %all-reduce.5.cloned.1.call-update) | async-done | bytes 3145744 | tf_op jit(solution)/shard_map/psum | solution.py:115
  351.7 8.0 %fusion.10 = bf16[2,1024,512]{2,1,0:T(8,128)(2,1)} fusion(s32[1024]{0:T(1024)S(1)} %copy-done.14, f32[2,1024,512]{2,1,0:T(8,128)} %get-tuple-element.31, f32[2,1024,512]{2,1,0:T(8,128)} %copy-done.5), kind=kOutput, calls=%fused_computation.16 | convolution fusion | flops 2162163712 | bytes 10489856 | tf_op jit(solution)/shard_map/cn,scd->snd/dot_general | solution.py:34
  359.6 23.5 %all-reduce.7.cloned.1.call-done = (f32[512,512]{0,1:T(8,128)}, f32[512,512]{0,1:T(8,128)}, f32[512,512]{0,1:T(8,128)}) async-done(((f32[512,512]{0,1:T(8,128)}, f32[512,512]{0,1:T(8,128)}, f32[512,512]{0,1:T(8,128)}), (f32[512,512]{0,1:T(8,128)}, f32[512,512]{0,1:T(8,128)}, f32[512,512]{0,1:T(8,128)})) %all-reduce.7.cloned.1.call-update) | async-done | bytes 3145744 | tf_op jit(solution)/shard_map/psum | solution.py:115
  383.1 1.8 broadcast_multiply_fusion
  384.9 1.3 copy.73
  386.2 1.3 copy.74
  387.5 1.3 broadcast_multiply_fusion.2
  388.9 1.3 copy.72
  (42 shorter events, 3.5 us)
Async XLA Ops:
  7.2 29.9 %copy-start = (bf16[32,128,128]{2,1,0:T(8,128)(2,1)S(1)}, bf16[32,128,128]{2,1,0:T(8,128)(2,1)}, u32[]{:S(2)}) copy-start(bf16[32,128,128]{2,1,0:T(8,128)(2,1)} %param.12) | copy-start | bytes 3145732
  7.2 11.7 %copy-start.2 = (bf16[2,1024,512]{2,1,0:T(8,128)(2,1)S(1)}, bf16[2,1024,512]{2,1,0:T(8,128)(2,1)}, u32[]{:S(2)}) copy-start(bf16[2,1024,512]{2,1,0:T(8,128)(2,1)} %param.11) | copy-start | bytes 6291460
  7.2 344.4 %all-reduce.5.cloned.1.call-start = ((), (), s32[]{:S(2)}) async-start(), calls=%async_computation | async-start | bytes 6291456 | tf_op jit(solution)/shard_map/psum | solution.py:115
  7.2 12.8 %copy-start.9 = (bf16[512,512]{1,0:T(8,128)(2,1)S(1)}, bf16[512,512]{1,0:T(8,128)(2,1)}, u32[]{:S(2)}) copy-start(bf16[512,512]{1,0:T(8,128)(2,1)} %param.19) | copy-start | bytes 1572868
  10.5 14.6 %collective-permute-start = (bf16[2,2,128,512]{3,1,2,0:T(2,128)(2,1)S(1)}, bf16[2,2,128,512]{3,1,2,0:T(2,128)(2,1)S(1)}, u32[]{:S(2)}, u32[]{:S(2)}) collective-permute-start(bf16[2,2,128,512]{3,1,2,0:T(2,128)(2,1)S(1)} %fusion.35), channel_id=1, source_target_pairs={{0,2},{2,4},{4,6},{6,8},{8,10},{10,12},{12,14},{14,16},{16,18},{18... | collective-permute-start | bytes 1572872 | tf_op jit(solution)/shard_map/ppermute | solution.py:11
  17.6 14.4 %collective-permute-start.1 = (bf16[2,2,128,512]{3,1,2,0:T(2,128)(2,1)S(1)}, bf16[2,2,128,512]{3,1,2,0:T(2,128)(2,1)S(1)}, u32[]{:S(2)}, u32[]{:S(2)}) collective-permute-start(bf16[2,2,128,512]{3,1,2,0:T(2,128)(2,1)S(1)} %fusion.36), channel_id=1, source_target_pairs={{2,0},{4,2},{6,4},{8,6},{10,8},{12,10},{14,12},{16,14},{18,16},{20... | collective-permute-start | bytes 1572872 | tf_op jit(solution)/shard_map/ppermute | solution.py:11
  20.1 11.9 %copy-start.15 = (s32[32]{0:T(128)S(1)}, s32[32]{0:T(128)}, u32[]{:S(2)}) copy-start(s32[32]{0:T(128)} %param.14) | copy-start | bytes 388
  55.6 20.0 %copy-start.11 = (s32[32]{0:T(128)S(1)}, s32[32]{0:T(128)}, u32[]{:S(2)}) copy-start(s32[32]{0:T(128)} %param.13) | copy-start | bytes 388
  75.6 11.6 %copy-start.10 = (bf16[512,512]{1,0:T(8,128)(2,1)S(1)}, bf16[512,512]{1,0:T(8,128)(2,1)}, u32[]{:S(2)}) copy-start(bf16[512,512]{1,0:T(8,128)(2,1)} %param.20) | copy-start | bytes 1572868
  85.2 2.9 copy-start.3
  85.9 1.3 copy-start.4
  88.1 1.3 copy-start.14
  89.4 5.5 %copy-start.5 = (f32[2,1024,512]{2,1,0:T(8,128)}, f32[2,1024,512]{2,1,0:T(8,128)S(1)}, u32[]{:S(2)}) copy-start(f32[2,1024,512]{2,1,0:T(8,128)S(1)} %convolution_add_fusion) | copy-start | bytes 12582916
  89.4 6.7 %copy-start.12 = (bf16[2,1024,512]{2,1,0:T(8,128)(2,1)S(1)}, bf16[2,1024,512]{2,1,0:T(8,128)(2,1)}, u32[]{:S(2)}) copy-start(bf16[2,1024,512]{2,1,0:T(8,128)(2,1)} %param.18) | copy-start | bytes 6291460
  94.9 45.6 %collective-permute-start.2 = (bf16[2,1024,512]{1,2,0:T(8,128)(2,1)}, bf16[2,1024,512]{1,2,0:T(8,128)(2,1)}, u32[]{:S(2)}, u32[]{:S(2)}) collective-permute-start(bf16[2,1024,512]{1,2,0:T(8,128)(2,1)} %get-tuple-element.26), channel_id=1, source_target_pairs={{0,2},{2,0},{4,6},{6,4},{8,10},{10,8},{12,14},{14,12},{16,18},{18,... | collective-permute-start | bytes 6291464 | tf_op jit(solution)/shard_map/ppermute | solution.py:17
  101.2 84.2 %collective-permute-start.3 = (bf16[2,1024,512]{2,1,0:T(8,128)(2,1)}, bf16[2,1024,512]{2,1,0:T(8,128)(2,1)}, u32[]{:S(2)}, u32[]{:S(2)}) collective-permute-start(bf16[2,1024,512]{2,1,0:T(8,128)(2,1)} %get-tuple-element.28), channel_id=1, source_target_pairs={{0,2},{2,0},{4,6},{6,4},{8,10},{10,8},{12,14},{14,12},{16,18},{18,... | collective-permute-start | bytes 6291464 | tf_op jit(solution)/shard_map/ppermute | solution.py:17
  140.4 44.9 %copy-start.13 = (bf16[512,512]{1,0:T(8,128)(2,1)S(1)}, bf16[512,512]{1,0:T(8,128)(2,1)}, u32[]{:S(2)}) copy-start(bf16[512,512]{1,0:T(8,128)(2,1)} %param.21) | copy-start | bytes 1572868
  140.4 44.9 %copy-start.17 = (f32[1024,2,512]{2,0,1:T(8,128)S(1)}, f32[1024,2,512]{2,0,1:T(8,128)}, u32[]{:S(2)}) copy-start(f32[1024,2,512]{2,0,1:T(8,128)} %get-tuple-element.29) | copy-start | bytes 12582916
  144.2 47.9 %copy-start.7 = (bf16[2,1024,512]{1,2,0:T(8,128)(2,1)}, bf16[2,1024,512]{1,2,0:T(8,128)(2,1)S(1)}, u32[]{:S(2)}) copy-start(bf16[2,1024,512]{1,2,0:T(8,128)(2,1)S(1)} %fusion.12) | copy-start | bytes 6291460
  200.2 4.6 %copy-start.6 = (bf16[2,1024,512]{2,1,0:T(8,128)(2,1)S(1)}, bf16[2,1024,512]{2,1,0:T(8,128)(2,1)}, u32[]{:S(2)}) copy-start(bf16[2,1024,512]{2,1,0:T(8,128)(2,1)} %fusion.7) | copy-start | bytes 6291460
  204.9 2.3 copy-start.8
  204.9 2.3 copy-start.16
  208.9 174.3 %all-reduce.7.cloned.1.call-start = ((), (), s32[]{:S(2)}) async-start(), calls=%async_computation.1 | async-start | bytes 6291456 | tf_op jit(solution)/shard_map/psum | solution.py:115
  384.9 5.3 %copy-start.1 = (bf16[32,128,128]{2,1,0:T(8,128)(2,1)S(1)}, bf16[32,128,128]{2,1,0:T(8,128)(2,1)}, u32[]{:S(2)}) copy-start(bf16[32,128,128]{2,1,0:T(8,128)(2,1)} %param.12) | copy-start | bytes 3145732
Sparse Core Ops, SparseCore 0:
  209.0 142.5 all-reduce.4
  354.4 28.6 all-reduce.6
